TPU v7x, 128 devices: a whole 4x4x4 slice. The times are simulated.
128 devices in a mesh: cluster: 16 (over y, x_lo, core), blk: 8 (over x_hi, z).
Axes of the slice: x: 4 (x_hi: 2, x_lo: 2; x = x_hi * 2 + x_lo), y: 4, z: 4, core: 2. Of those that a mesh axis runs over, the one named last changes fastest.
Arguments:
- embeds: bfloat16 [4096, 32, 128], P(('cluster', 'blk')), may hold values from -7 to 7
- labels: int32 [4096, 1], P(('cluster', 'blk')), may hold values from 0 to 15, as said below
- keep: int32 [4096], P(('cluster', 'blk')), may hold values 0 or 1
Outputs:
- dup_score: float32 [4096], P(('cluster', 'blk'))
Inputs may be any that keep to these rules, and one draw needn't show every extreme that they name: `labels`: at most 4 prompts of one device carry the same label, and on every device some label is carried by exactly 4 of its prompts.
All inputs are finite; a program needn't handle non-finite values. No bound on the sum of `keep` on one device may be relied on, other than what follows from the above.
Results may differ from a plain program's by a relative error of at most 0.0003.
Values may be sent and summed in bfloat16 or wider, within the bound.
A program may use at most 64 MiB of HBM per device.

v0:
```python
import jax
import jax.numpy as jnp
from jax import lax
from jax.sharding import PartitionSpec as P

SLOTS = 64
group_size = 8


def pair_scores(residents, visitors):
    length = residents.shape[1]
    width = residents.shape[2]
    visiting = visitors.shape[0]
    flat_visitors = visitors.reshape(visiting * length, width)
    grouped = residents.reshape(residents.shape[0] // group_size, group_size * length, width)

    def one_group(queries):
        score_tile = lax.dot_general(
            queries, flat_visitors, (((1,), (1,)), ((), ())), preferred_element_type=jnp.float32
        )
        score_tile = score_tile.reshape(group_size, length, visiting, length)
        forward = jnp.sum(jnp.max(score_tile, axis=3), axis=1) / length
        return forward

    result = lax.map(one_group, grouped)
    return result.reshape(-1, visiting)


def body(embeds, labels, keep):
    clusters = lax.axis_size("cluster")
    slot_count = SLOTS
    capacity = slot_count // clusters
    label_list = labels[:, 0]
    onehot = (label_list[:, None] == jnp.arange(clusters, dtype=jnp.int32)[None, :]).astype(
        jnp.int32
    )
    slot_rank = jnp.sum((jnp.cumsum(onehot, axis=0) - onehot) * onehot, axis=1)
    slot_index = label_list * capacity + slot_rank
    keep_float = keep.astype(jnp.float32)
    outgoing = (
        jnp.zeros((slot_count, embeds.shape[1], embeds.shape[2]), jnp.bfloat16)
        .at[slot_index]
        .set(embeds)
    )
    outgoing_flags = (
        jnp.zeros((slot_count,), jnp.bfloat16).at[slot_index].set(keep.astype(jnp.bfloat16))
    )
    members, member_flags = (
        lax.all_to_all(outgoing, "cluster", split_axis=0, concat_axis=0, tiled=True),
        lax.all_to_all(outgoing_flags, "cluster", split_axis=0, concat_axis=0, tiled=True),
    )
    flags = member_flags.astype(jnp.float32)
    own_ids = lax.axis_index("blk") * slot_count + jnp.arange(slot_count, dtype=jnp.int32)
    visitors = lax.all_gather(members, "blk", axis=0, tiled=True)
    visitor_flags = lax.all_gather(member_flags, "blk", axis=0, tiled=True)
    other_ids = jnp.arange(visitors.shape[0], dtype=jnp.int32)
    weights = (own_ids[:, None] != other_ids[None, :]).astype(jnp.float32) * visitor_flags.astype(
        jnp.float32
    )[None, :]
    forward = pair_scores(members, visitors)
    sums = jnp.sum(forward * weights, axis=1)
    counts = jnp.sum(weights, axis=1)
    score = jnp.where(flags > 0, sums / jnp.maximum(counts, 1.0), 0.0)
    returned = lax.all_to_all(score, "cluster", split_axis=0, concat_axis=0, tiled=True)
    return returned[slot_index] * keep_float


def solution(mesh):
    return jax.shard_map(
        body,
        mesh=mesh,
        in_specs=(
            P(("cluster", "blk"), None, None),
            P(("cluster", "blk"), None),
            P(("cluster", "blk")),
        ),
        out_specs=P(("cluster", "blk")),
        check_vma=False,
    )
```

profile of v0, /device:TPU:1, one launch (start us, length us, event | category | flops | bytes accessed | tf_op | source)
XLA Modules:
  0.0 191.4 jit_solution(1213588134446596878)
XLA Ops:
  6.5 0.0 all-gather.2.cloned.1.call-start
  6.5 0.7 fusion.6
  7.3 0.1 reduce_window_sum.11
  7.3 0.8 select_reduce_fusion.1
  8.2 0.7 fusion.7
  8.8 0.1 broadcast_in_dim.11
  8.9 2.8 %scatter_fusion = bf16[64,32,128]{2,1,0:T(8,128)(2,1)S(1)} fusion(bf16[64,32,128]{2,1,0:T(8,128)(2,1)S(1)} %broadcast_in_dim.11, s32[32]{0:T(128)S(1)} %fusion.7, bf16[32,32,128]{2,1,0:T(8,128)(2,1)} %param.5), kind=kCustom, calls=%fused_computation.2 | custom fusion | bytes 786560 | tf_op jit(solution)/shard_map/scatter | solution.py:43
  11.7 16.6 %all_to_all.27 = bf16[64,32,128]{2,1,0:T(8,128)(2,1)} all-to-all(bf16[64,32,128]{2,1,0:T(8,128)(2,1)S(1)} %scatter_fusion), channel_id=1, replica_groups=mesh['cluster'=16,'blk'=8] {'cluster'}, dimensions={0} | all-to-all | bytes 1048576 | tf_op jit(solution)/shard_map/all_to_all | solution.py:49
  28.4 0.0 all-gather.2.cloned.1.call-update
  28.4 0.7 convert_element_type.18
  29.0 0.8 scatter_custom_fusion
  29.8 0.7 all_to_all.23
  30.5 4.3 %all-to-all-start = ((bf16[16,4,1]{1,2,0:T(2,128)(2,1)}), bf16[16,4,1]{1,2,0:T(2,128)(2,1)S(1)}, u32[]{:S(2)}, u32[]{:S(2)}) async-start(bf16[16,4,1]{1,2,0:T(2,128)(2,1)} %all_to_all.23), calls=%async_computation | async-start | bytes 16384 | tf_op jit(solution)/shard_map/all_to_all | solution.py:50
  34.9 1.3 dynamic-slice
  36.8 3.6 %all-to-all-done = bf16[16,4,1]{1,2,0:T(2,128)(2,1)S(1)} async-done(((bf16[16,4,1]{1,2,0:T(2,128)(2,1)}), bf16[16,4,1]{1,2,0:T(2,128)(2,1)S(1)}, u32[]{:S(2)}, u32[]{:S(2)}) %all-to-all-start) | async-done | bytes 160 | tf_op jit(solution)/shard_map/all_to_all | solution.py:50
  40.4 0.1 reshape.94
  40.5 0.2 dynamic-update-slice
  40.8 21.5 %all-reduce = bf16[512]{0:T(512)(128)(2,1)S(1)} all-reduce(bf16[512]{0:T(512)(128)(2,1)S(1)} %dynamic-update-slice), channel_id=1, replica_groups=mesh['cluster'=16,'blk'=8] {'blk'}, use_global_device_ids=true, to_apply=%add | all-reduce | flops 512 | bytes 2048
  62.3 0.2 select_reduce_fusion
  62.5 0.1 max.18
  62.6 37.5 %all-gather.2.cloned.1.call-done = bf16[512,32,128]{2,1,0:T(8,128)(2,1)} async-done(((bf16[64,32,128]{2,1,0:T(8,128)(2,1)}), bf16[512,32,128]{2,1,0:T(8,128)(2,1)}) %all-gather.2.cloned.1.call-update) | async-done | bytes 4194320 | tf_op jit(solution)/shard_map/all_gather | solution.py:54
  100.0 0.0 copy-start
  100.0 70.3 %while.11 = (s32[]{:T(128)}, f32[8,8,512]{2,1,0:T(8,128)S(1)}, bf16[8,256,128]{2,1,0:T(8,128)(2,1)}, bf16[16384,128]{1,0:T(8,128)(2,1)}) while((s32[]{:T(128)}, f32[8,8,512]{2,1,0:T(8,128)S(1)}, bf16[8,256,128]{2,1,0:T(8,128)(2,1)}, bf16[16384,128]{1,0:T(8,128)(2,1)}) %tuple.27), condition=%wide.region_7.8_spmd.clone, body=%wide.region_4.7_spmd.sunk.clone | while | flops 1077936128 | bytes 5488705 | solution.py:25
  100.0 0.9 constant_dynamic-slice_fusion.3
  100.9 7.8 %fusion.19 = f32[8,32,512]{2,1,0:T(8,128)S(1)} fusion(bf16[8,32,128,1]{2,1,3,0:T(8,128)(2,1)S(1)} %bitcast.42, bf16[512,32,128]{2,1,0:T(8,128)(2,1)} %bitcast.46), kind=kOutput, calls=%fused_computation.6.clone.1.clone | convolution fusion | flops 1077805056 | bytes 4784128 | tf_op jit(solution)/shard_map/while/body/eval_jaxpr/dot_general | solution.py:18
  108.7 0.1 reduce_sum.50
  108.8 0.8 constant_dynamic-slice_fusion.3
  109.7 7.8 %fusion.19 = f32[8,32,512]{2,1,0:T(8,128)S(1)} fusion(bf16[8,32,128,1]{2,1,3,0:T(8,128)(2,1)S(1)} %bitcast.42, bf16[512,32,128]{2,1,0:T(8,128)(2,1)} %bitcast.46), kind=kOutput, calls=%fused_computation.6.clone.1.clone | convolution fusion | flops 1077805056 | bytes 4784128 | tf_op jit(solution)/shard_map/while/body/eval_jaxpr/dot_general | solution.py:18
  117.5 0.1 reduce_sum.50
  117.6 0.8 constant_dynamic-slice_fusion.3
  118.5 7.8 %fusion.19 = f32[8,32,512]{2,1,0:T(8,128)S(1)} fusion(bf16[8,32,128,1]{2,1,3,0:T(8,128)(2,1)S(1)} %bitcast.42, bf16[512,32,128]{2,1,0:T(8,128)(2,1)} %bitcast.46), kind=kOutput, calls=%fused_computation.6.clone.1.clone | convolution fusion | flops 1077805056 | bytes 4784128 | tf_op jit(solution)/shard_map/while/body/eval_jaxpr/dot_general | solution.py:18
  126.3 0.1 reduce_sum.50
  126.4 0.8 constant_dynamic-slice_fusion.3
  127.2 7.8 %fusion.19 = f32[8,32,512]{2,1,0:T(8,128)S(1)} fusion(bf16[8,32,128,1]{2,1,3,0:T(8,128)(2,1)S(1)} %bitcast.42, bf16[512,32,128]{2,1,0:T(8,128)(2,1)} %bitcast.46), kind=kOutput, calls=%fused_computation.6.clone.1.clone | convolution fusion | flops 1077805056 | bytes 4784128 | tf_op jit(solution)/shard_map/while/body/eval_jaxpr/dot_general | solution.py:18
  135.1 0.1 reduce_sum.50
  135.2 0.8 constant_dynamic-slice_fusion.3
  136.0 7.8 %fusion.19 = f32[8,32,512]{2,1,0:T(8,128)S(1)} fusion(bf16[8,32,128,1]{2,1,3,0:T(8,128)(2,1)S(1)} %bitcast.42, bf16[512,32,128]{2,1,0:T(8,128)(2,1)} %bitcast.46), kind=kOutput, calls=%fused_computation.6.clone.1.clone | convolution fusion | flops 1077805056 | bytes 4784128 | tf_op jit(solution)/shard_map/while/body/eval_jaxpr/dot_general | solution.py:18
  143.9 0.1 reduce_sum.50
  144.0 0.8 constant_dynamic-slice_fusion.3
  144.8 7.8 %fusion.19 = f32[8,32,512]{2,1,0:T(8,128)S(1)} fusion(bf16[8,32,128,1]{2,1,3,0:T(8,128)(2,1)S(1)} %bitcast.42, bf16[512,32,128]{2,1,0:T(8,128)(2,1)} %bitcast.46), kind=kOutput, calls=%fused_computation.6.clone.1.clone | convolution fusion | flops 1077805056 | bytes 4784128 | tf_op jit(solution)/shard_map/while/body/eval_jaxpr/dot_general | solution.py:18
  152.6 0.1 reduce_sum.50
  152.7 0.8 constant_dynamic-slice_fusion.3
  153.6 7.8 %fusion.19 = f32[8,32,512]{2,1,0:T(8,128)S(1)} fusion(bf16[8,32,128,1]{2,1,3,0:T(8,128)(2,1)S(1)} %bitcast.42, bf16[512,32,128]{2,1,0:T(8,128)(2,1)} %bitcast.46), kind=kOutput, calls=%fused_computation.6.clone.1.clone | convolution fusion | flops 1077805056 | bytes 4784128 | tf_op jit(solution)/shard_map/while/body/eval_jaxpr/dot_general | solution.py:18
  161.4 0.1 reduce_sum.50
  161.5 0.8 constant_dynamic-slice_fusion.3
  162.4 7.8 %fusion.19 = f32[8,32,512]{2,1,0:T(8,128)S(1)} fusion(bf16[8,32,128,1]{2,1,3,0:T(8,128)(2,1)S(1)} %bitcast.42, bf16[512,32,128]{2,1,0:T(8,128)(2,1)} %bitcast.46), kind=kOutput, calls=%fused_computation.6.clone.1.clone | convolution fusion | flops 1077805056 | bytes 4784128 | tf_op jit(solution)/shard_map/while/body/eval_jaxpr/dot_general | solution.py:18
  170.2 0.1 reduce_sum.50
  170.3 0.2 multiply_reduce_fusion
  170.5 0.1 reduce_sum.43
  170.5 0.6 divide_select_fusion
  171.1 5.4 %all-to-all-start.2 = ((f32[16,4,1]{1,2,0:T(1,128)}), f32[16,4,1]{1,2,0:T(1,128)S(1)}, u32[]{:S(2)}, u32[]{:S(2)}) async-start(f32[16,4,1]{1,2,0:T(1,128)} %bitcast.12), calls=%async_computation.2 | async-start | bytes 16384 | tf_op jit(solution)/shard_map/all_to_all | solution.py:64
  176.5 5.5 %all-to-all-done.2 = f32[16,4,1]{1,2,0:T(1,128)S(1)} async-done(((f32[16,4,1]{1,2,0:T(1,128)}), f32[16,4,1]{1,2,0:T(1,128)S(1)}, u32[]{:S(2)}, u32[]{:S(2)}) %all-to-all-start.2) | async-done | bytes 288 | tf_op jit(solution)/shard_map/all_to_all | solution.py:64
  182.0 0.5 broadcast.75
  182.5 0.7 reduce.5
  183.2 0.1 all_to_all.22
  183.3 0.7 gather_fusion
  184.0 0.0 copy-done
  184.0 0.5 convert_multiply_fusion
  (16 shorter events, 0.1 us)
Async XLA Ops:
  6.5 93.5 %all-gather.2.cloned.1.call-start = ((), (), s32[]{:S(2)}) async-start(), calls=%async_computation.3 | async-start | bytes 4718592 | tf_op jit(solution)/shard_map/all_gather | solution.py:54
  30.5 9.9 %all-to-all-start = ((bf16[16,4,1]{1,2,0:T(2,128)(2,1)}), bf16[16,4,1]{1,2,0:T(2,128)(2,1)S(1)}, u32[]{:S(2)}, u32[]{:S(2)}) async-start(bf16[16,4,1]{1,2,0:T(2,128)(2,1)} %all_to_all.23), calls=%async_computation | async-start | bytes 16384 | tf_op jit(solution)/shard_map/all_to_all | solution.py:50
  100.0 84.0 %copy-start = (s32[32]{0:T(128)S(1)}, s32[32]{0:T(128)}, u32[]{:S(2)}) copy-start(s32[32]{0:T(128)} %param.7) | copy-start | bytes 388
  171.1 10.9 %all-to-all-start.2 = ((f32[16,4,1]{1,2,0:T(1,128)}), f32[16,4,1]{1,2,0:T(1,128)S(1)}, u32[]{:S(2)}, u32[]{:S(2)}) async-start(f32[16,4,1]{1,2,0:T(1,128)} %bitcast.12), calls=%async_computation.2 | async-start | bytes 16384 | tf_op jit(solution)/shard_map/all_to_all | solution.py:64
Sparse Core Ops, SparseCore 0:
  28.5 71.4 all-gather.1
where the time goes:
time: 192 us; the launch traced here: 191 us
  matrix products  62.6 us (33%)
  waiting for transfers between devices  46.5 us (24%)
  blocking collectives  38.1 us (20%)
  local copies, waits for them, and re-layouts  14.3 us (7%)
  between operations  14.1 us (7%)
  starting transfers between devices  9.73 us (5%)
  other arithmetic  5.72 us (3%)
    dot_general x8, matrix products, one_group(): lax.dot_general(queries, flat_visitors, (((1,), (1,)), ((), ())), preferr...  62.6 us
    all_gather x1, waiting for transfers between devices, body(): visitors = lax.all_gather(members, 'blk', axis=0, tiled=True)  37.5 us
    unnamed x1, blocking collectives  21.5 us
    all_to_all x1, blocking collectives, body(): lax.all_to_all(outgoing, 'cluster', split_axis=0, concat_axis=0, tiled=True)  16.6 us
    dynamic_slice x8, local copies, waits for them, and re-layouts, pair_scores(): result = lax.map(one_group, grouped)  6.8 us
    all_to_all x1, waiting for transfers between devices, body(): lax.all_to_all(score, 'cluster', split_axis=0, concat_axis=0, tiled=True)  5.47 us
    all_to_all x1, starting transfers between devices, body(): lax.all_to_all(score, 'cluster', split_axis=0, concat_axis=0, tiled=True)  5.39 us
    all_to_all x1, starting transfers between devices, body(): lax.all_to_all(outgoing_flags, 'cluster', split_axis=0, concat_axis=0, ti...  4.34 us
  transfers between devices with their start and end apart: 3, of which 3 were waited for; matrix products, arithmetic and copies ran while one was open for 2% of the time, Pallas kernels for 0%

commit v1 on v0

--- a/solution.py
+++ b/solution.py
@@ -5,6 +5,13 @@
 
 SLOTS = 64
 group_size = 8
+
+
+def swapped_in(value, axis, dim):
+    devices = lax.axis_size(axis)
+    blocks = jnp.stack([value for _ in range(devices)])
+    blocks = lax.all_to_all(blocks, axis, split_axis=0, concat_axis=0)
+    return jnp.concatenate(blocks, axis=dim)
 
 
 def pair_scores(residents, visitors):
@@ -51,7 +58,7 @@
     )
     flags = member_flags.astype(jnp.float32)
     own_ids = lax.axis_index("blk") * slot_count + jnp.arange(slot_count, dtype=jnp.int32)
-    visitors = lax.all_gather(members, "blk", axis=0, tiled=True)
+    visitors = swapped_in(members, "blk", 0)
     visitor_flags = lax.all_gather(member_flags, "blk", axis=0, tiled=True)
     other_ids = jnp.arange(visitors.shape[0], dtype=jnp.int32)
     weights = (own_ids[:, None] != other_ids[None, :]).astype(jnp.float32) * visitor_flags.astype(

time: 192 us -> 179 us (0.932)
  waiting for transfers between devices: 46.5 us -> 8.1 us
  blocking collectives: 38.1 us -> 69.9 us
  between operations: 14.1 us -> 0.68 us
  starting transfers between devices: 9.73 us -> 22.3 us
  local copies, waits for them, and re-layouts: 14.3 us -> 9.5 us
    all_gather x1 -> x0, waiting for transfers between devices: 37.5 us -> none  [body(): visitors = lax.all_gather(members, 'blk', axis=0, tiled=True)]
    unnamed x1, blocking collectives: 21.5 us -> 57.1 us
    all_to_all x0 -> x1, starting transfers between devices: none -> 7.33 us  [swapped_in(): blocks = lax.all_to_all(blocks, axis, split_axis=0, concat_axis=0)]
    dynamic_slice x8, local copies, waits for them, and re-layouts: 6.8 us -> 0.09 us  [pair_scores(): result = lax.map(one_group, grouped)]
    all_to_all x1, blocking collectives: 16.6 us -> 12.8 us  [body(): lax.all_to_all(outgoing, 'cluster', split_axis=0, concat_axis=0, tiled=True)]
    another operation x0 -> x1, local copies, waits for them, and re-layouts: none -> 2.69 us  [swapped_in(): blocks = jnp.stack([value for _ in range(devices)])]
    all_to_all x1, starting transfers between devices: 5.39 us -> 8.07 us  [body(): lax.all_to_all(score, 'cluster', split_axis=0, concat_axis=0, tiled=True)]
    all_to_all x1, starting transfers between devices: 4.34 us -> 6.91 us  [body(): lax.all_to_all(outgoing_flags, 'cluster', split_axis=0, concat_axis=0, ti...]
  transfers between devices with their start and end apart: 3 -> 3, of which waited for: 3 -> 2; matrix products, arithmetic and copies ran while one was open for 2% -> 2% of each run, Pallas kernels for 0% -> 0%
where the time goes in v1:
time: 179 us; the launch traced here: 178 us
  blocking collectives  69.9 us (39%)
  matrix products  61.7 us (34%)
  starting transfers between devices  22.3 us (12%)
  local copies, waits for them, and re-layouts  9.5 us (5%)
  waiting for transfers between devices  8.1 us (5%)
  other arithmetic  5.72 us (3%)
    dot_general x8, matrix products, one_group(): lax.dot_general(queries, flat_visitors, (((1,), (1,)), ((), ())), preferr...  61.7 us
    unnamed x1, blocking collectives  57.1 us
    all_to_all x1, blocking collectives, body(): lax.all_to_all(outgoing, 'cluster', split_axis=0, concat_axis=0, tiled=True)  12.8 us
    all_to_all x1, starting transfers between devices, body(): lax.all_to_all(score, 'cluster', split_axis=0, concat_axis=0, tiled=True)  8.07 us
    all_to_all x1, starting transfers between devices, swapped_in(): blocks = lax.all_to_all(blocks, axis, split_axis=0, concat_axis=0)  7.33 us
    all_to_all x1, starting transfers between devices, body(): lax.all_to_all(outgoing_flags, 'cluster', split_axis=0, concat_axis=0, ti...  6.91 us
    all_to_all x1, waiting for transfers between devices, body(): lax.all_to_all(score, 'cluster', split_axis=0, concat_axis=0, tiled=True)  5.53 us
  transfers between devices with their start and end apart: 3, of which 2 were waited for; matrix products, arithmetic and copies ran while one was open for 2% of the time, Pallas kernels for 0%

profile of v1, /device:TPU:1, one launch (start us, length us, event | category | flops | bytes accessed | tf_op | source)
XLA Modules:
  0.0 178.3 jit_solution(6578151583845348035)
XLA Ops:
  0.0 0.7 fusion.6
  0.7 0.1 reduce_window_sum.11
  0.8 0.8 select_reduce_fusion.1
  1.6 0.7 fusion.7
  2.3 0.7 convert_element_type.18
  2.9 0.8 scatter_custom_fusion
  3.7 0.7 all_to_all.27
  4.4 6.9 %all-to-all-start = ((bf16[16,4,1]{1,2,0:T(2,128)(2,1)}), bf16[16,4,1]{1,2,0:T(2,128)(2,1)S(1)}, u32[]{:S(2)}, u32[]{:S(2)}) async-start(bf16[16,4,1]{1,2,0:T(2,128)(2,1)} %all_to_all.27), calls=%async_computation | async-start | bytes 16384 | tf_op jit(solution)/shard_map/all_to_all | solution.py:57
  11.3 0.1 broadcast_in_dim.11
  11.4 2.8 %scatter_fusion = bf16[64,32,128]{2,1,0:T(8,128)(2,1)S(1)} fusion(bf16[64,32,128]{2,1,0:T(8,128)(2,1)S(1)} %broadcast_in_dim.11, s32[32]{0:T(128)S(1)} %fusion.7, bf16[32,32,128]{2,1,0:T(8,128)(2,1)} %param.5), kind=kCustom, calls=%fused_computation.2 | custom fusion | bytes 786560 | tf_op jit(solution)/shard_map/scatter | solution.py:50
  14.2 2.6 %all-to-all-done = bf16[16,4,1]{1,2,0:T(2,128)(2,1)S(1)} async-done(((bf16[16,4,1]{1,2,0:T(2,128)(2,1)}), bf16[16,4,1]{1,2,0:T(2,128)(2,1)S(1)}, u32[]{:S(2)}, u32[]{:S(2)}) %all-to-all-start) | async-done | bytes 160 | tf_op jit(solution)/shard_map/all_to_all | solution.py:57
  16.8 12.8 %all_to_all.32 = bf16[64,32,128]{2,1,0:T(8,128)(2,1)S(1)} all-to-all(bf16[64,32,128]{2,1,0:T(8,128)(2,1)S(1)} %scatter_fusion), channel_id=1, replica_groups=mesh['cluster'=16,'blk'=8] {'cluster'}, dimensions={0} | all-to-all | bytes 1048576 | tf_op jit(solution)/shard_map/all_to_all | solution.py:56
  29.6 2.7 %stack.2 = bf16[8,64,32,128]{3,2,1,0:T(8,128)(2,1)} broadcast(bf16[64,32,128]{2,1,0:T(8,128)(2,1)S(1)} %all_to_all.32), dimensions={1,2,3} | broadcast | bytes 4718592 | tf_op jit(solution)/shard_map/stack | solution.py:12
  32.3 0.0 copy-start.1
  32.3 7.3 %all-to-all-start.2 = ((bf16[8,64,32,128]{3,2,1,0:T(8,128)(2,1)}), bf16[8,64,32,128]{3,2,1,0:T(8,128)(2,1)}, u32[]{:S(2)}, u32[]{:S(2)}) async-start(bf16[8,64,32,128]{3,2,1,0:T(8,128)(2,1)} %stack.2), calls=%async_computation.2 | async-start | bytes 8388608 | tf_op jit(solution)/shard_map/all_to_all | solution.py:13
  39.7 0.0 copy-done.1
  39.7 0.6 dynamic-slice
  40.9 0.1 reshape.92
  41.0 0.2 dynamic-update-slice
  41.2 57.1 %all-reduce = bf16[512]{0:T(512)(128)(2,1)S(1)} all-reduce(bf16[512]{0:T(512)(128)(2,1)S(1)} %dynamic-update-slice), channel_id=1, replica_groups=mesh['cluster'=16,'blk'=8] {'blk'}, use_global_device_ids=true, to_apply=%add | all-reduce | flops 512 | bytes 2048
  98.3 0.2 select_reduce_fusion
  98.5 0.1 max.18
  98.6 0.0 all-to-all-done.2
  98.6 0.0 copy-start
  98.6 62.7 %while.11 = (s32[]{:T(128)}, f32[8,8,512]{2,1,0:T(8,128)S(1)}, bf16[8,256,128]{2,1,0:T(8,128)(2,1)S(1)}, bf16[16384,128]{1,0:T(8,128)(2,1)}) while((s32[]{:T(128)}, f32[8,8,512]{2,1,0:T(8,128)S(1)}, bf16[8,256,128]{2,1,0:T(8,128)(2,1)S(1)}, bf16[16384,128]{1,0:T(8,128)(2,1)}) %tuple.24), condition=%wide.region_7.8_spmd.clone, body=%wide.region_4.7_spmd.sunk.clone | while | flops 1077936128 | bytes 5488705 | solution.py:32
  98.6 7.7 %fusion.19 = f32[8,32,512]{2,1,0:T(8,128)S(1)} fusion(bf16[8,32,128,1]{2,1,3,0:T(8,128)(2,1)S(1)} %bitcast.42, bf16[512,32,128]{2,1,0:T(8,128)(2,1)} %bitcast.40), kind=kOutput, calls=%fused_computation.6.clone.1.clone | convolution fusion | flops 1077805056 | bytes 4784128 | tf_op jit(solution)/shard_map/while/body/eval_jaxpr/dot_general | solution.py:25
  106.4 0.1 reduce_sum.50
  106.5 7.7 %fusion.19 = f32[8,32,512]{2,1,0:T(8,128)S(1)} fusion(bf16[8,32,128,1]{2,1,3,0:T(8,128)(2,1)S(1)} %bitcast.42, bf16[512,32,128]{2,1,0:T(8,128)(2,1)} %bitcast.40), kind=kOutput, calls=%fused_computation.6.clone.1.clone | convolution fusion | flops 1077805056 | bytes 4784128 | tf_op jit(solution)/shard_map/while/body/eval_jaxpr/dot_general | solution.py:25
  114.2 0.1 reduce_sum.50
  114.3 7.7 %fusion.19 = f32[8,32,512]{2,1,0:T(8,128)S(1)} fusion(bf16[8,32,128,1]{2,1,3,0:T(8,128)(2,1)S(1)} %bitcast.42, bf16[512,32,128]{2,1,0:T(8,128)(2,1)} %bitcast.40), kind=kOutput, calls=%fused_computation.6.clone.1.clone | convolution fusion | flops 1077805056 | bytes 4784128 | tf_op jit(solution)/shard_map/while/body/eval_jaxpr/dot_general | solution.py:25
  122.0 0.1 reduce_sum.50
  122.2 7.7 %fusion.19 = f32[8,32,512]{2,1,0:T(8,128)S(1)} fusion(bf16[8,32,128,1]{2,1,3,0:T(8,128)(2,1)S(1)} %bitcast.42, bf16[512,32,128]{2,1,0:T(8,128)(2,1)} %bitcast.40), kind=kOutput, calls=%fused_computation.6.clone.1.clone | convolution fusion | flops 1077805056 | bytes 4784128 | tf_op jit(solution)/shard_map/while/body/eval_jaxpr/dot_general | solution.py:25
  129.9 0.1 reduce_sum.50
  130.0 7.7 %fusion.19 = f32[8,32,512]{2,1,0:T(8,128)S(1)} fusion(bf16[8,32,128,1]{2,1,3,0:T(8,128)(2,1)S(1)} %bitcast.42, bf16[512,32,128]{2,1,0:T(8,128)(2,1)} %bitcast.40), kind=kOutput, calls=%fused_computation.6.clone.1.clone | convolution fusion | flops 1077805056 | bytes 4784128 | tf_op jit(solution)/shard_map/while/body/eval_jaxpr/dot_general | solution.py:25
  137.7 0.1 reduce_sum.50
  137.8 7.7 %fusion.19 = f32[8,32,512]{2,1,0:T(8,128)S(1)} fusion(bf16[8,32,128,1]{2,1,3,0:T(8,128)(2,1)S(1)} %bitcast.42, bf16[512,32,128]{2,1,0:T(8,128)(2,1)} %bitcast.40), kind=kOutput, calls=%fused_computation.6.clone.1.clone | convolution fusion | flops 1077805056 | bytes 4784128 | tf_op jit(solution)/shard_map/while/body/eval_jaxpr/dot_general | solution.py:25
  145.6 0.1 reduce_sum.50
  145.7 7.7 %fusion.19 = f32[8,32,512]{2,1,0:T(8,128)S(1)} fusion(bf16[8,32,128,1]{2,1,3,0:T(8,128)(2,1)S(1)} %bitcast.42, bf16[512,32,128]{2,1,0:T(8,128)(2,1)} %bitcast.40), kind=kOutput, calls=%fused_computation.6.clone.1.clone | convolution fusion | flops 1077805056 | bytes 4784128 | tf_op jit(solution)/shard_map/while/body/eval_jaxpr/dot_general | solution.py:25
  153.4 0.1 reduce_sum.50
  153.5 7.7 %fusion.19 = f32[8,32,512]{2,1,0:T(8,128)S(1)} fusion(bf16[8,32,128,1]{2,1,3,0:T(8,128)(2,1)S(1)} %bitcast.42, bf16[512,32,128]{2,1,0:T(8,128)(2,1)} %bitcast.40), kind=kOutput, calls=%fused_computation.6.clone.1.clone | convolution fusion | flops 1077805056 | bytes 4784128 | tf_op jit(solution)/shard_map/while/body/eval_jaxpr/dot_general | solution.py:25
  161.2 0.1 reduce_sum.50
  161.3 0.2 multiply_reduce_fusion
  161.5 0.1 reduce_sum.43
  161.6 0.6 divide_select_fusion
  162.2 8.1 %all-to-all-start.3 = ((f32[16,4,1]{1,2,0:T(1,128)}), f32[16,4,1]{1,2,0:T(1,128)S(1)}, u32[]{:S(2)}, u32[]{:S(2)}) async-start(f32[16,4,1]{1,2,0:T(1,128)} %bitcast.12), calls=%async_computation.3 | async-start | bytes 16384 | tf_op jit(solution)/shard_map/all_to_all | solution.py:71
  170.3 5.5 %all-to-all-done.3 = f32[16,4,1]{1,2,0:T(1,128)S(1)} async-done(((f32[16,4,1]{1,2,0:T(1,128)}), f32[16,4,1]{1,2,0:T(1,128)S(1)}, u32[]{:S(2)}, u32[]{:S(2)}) %all-to-all-start.3) | async-done | bytes 288 | tf_op jit(solution)/shard_map/all_to_all | solution.py:71
  175.8 0.5 broadcast.77
  176.3 0.7 reduce.5
  177.0 0.1 all_to_all.26
  177.1 0.7 gather_fusion
  177.8 0.0 copy-done
  177.8 0.5 convert_multiply_fusion
  (24 shorter events, 0.2 us)
Async XLA Ops:
  4.4 12.4 %all-to-all-start = ((bf16[16,4,1]{1,2,0:T(2,128)(2,1)}), bf16[16,4,1]{1,2,0:T(2,128)(2,1)S(1)}, u32[]{:S(2)}, u32[]{:S(2)}) async-start(bf16[16,4,1]{1,2,0:T(2,128)(2,1)} %all_to_all.27), calls=%async_computation | async-start | bytes 16384 | tf_op jit(solution)/shard_map/all_to_all | solution.py:57
  32.3 7.3 %copy-start.1 = (u32[128]{0:T(128)S(1)}, u32[128]{0:T(128)}, u32[]{:S(2)}) copy-start(u32[128]{0:T(128)} %constant.49) | copy-start | bytes 1540
  32.3 66.3 %all-to-all-start.2 = ((bf16[8,64,32,128]{3,2,1,0:T(8,128)(2,1)}), bf16[8,64,32,128]{3,2,1,0:T(8,128)(2,1)}, u32[]{:S(2)}, u32[]{:S(2)}) async-start(bf16[8,64,32,128]{3,2,1,0:T(8,128)(2,1)} %stack.2), calls=%async_computation.2 | async-start | bytes 8388608 | tf_op jit(solution)/shard_map/all_to_all | solution.py:13
  98.6 79.2 %copy-start = (s32[32]{0:T(128)S(1)}, s32[32]{0:T(128)}, u32[]{:S(2)}) copy-start(s32[32]{0:T(128)} %param.7) | copy-start | bytes 388
  162.2 13.6 %all-to-all-start.3 = ((f32[16,4,1]{1,2,0:T(1,128)}), f32[16,4,1]{1,2,0:T(1,128)S(1)}, u32[]{:S(2)}, u32[]{:S(2)}) async-start(f32[16,4,1]{1,2,0:T(1,128)} %bitcast.12), calls=%async_computation.3 | async-start | bytes 16384 | tf_op jit(solution)/shard_map/all_to_all | solution.py:71
